TPU v7x, 32 devices: a whole 2x2x4 slice. The times are simulated.
32 devices in a mesh: egrp: 2 (over x), space: 16 (over z, y, core).
Axes of the slice: x: 2, y: 2, z: 4, core: 2. Of those that a mesh axis runs over, the one named last changes fastest.
Arguments:
- dist: float32 [2, 1024, 64, 128], P(None, 'egrp', 'space'), may hold values from -12 to 12
- hist_x: bfloat16 [4, 2, 1024, 64, 128], P(None, None, 'egrp', 'space'), may hold values from -6 to 6
- hist_g: bfloat16 [4, 2, 1024, 64, 128], P(None, None, 'egrp', 'space'), may hold values from -12 to 12
- mobility: float32 [64, 128], P('space'), may hold values from 0.2 to 2
- region: int32 [64, 128], P('space'), may hold values from 0 to 3
- phonon_bins: int32 [4], replicated, may hold values from 48 to 64, as said below
- coupling: float32 [4], replicated, may hold values from 0.2 to 1.5
- hist_used: int32 [2, 4], replicated, may hold values 0 or 1
Outputs:
- drifted: float32 [2, 1024, 64, 128], P(None, 'egrp', 'space')
Inputs may be any that keep to these rules, and one draw needn't show every extreme that they name: `phonon_bins`: each value lies in 48 to 64; both ends occur.
All inputs are finite; a program needn't handle non-finite values.
Results may differ from a plain program's by a relative error of at most 0.0003.
Values sent between devices are 32-bit elements; how exact they have to be, the bound alone decides.
A program may use at most 128 MiB of HBM per device.

v0:
```python
import jax
import jax.numpy as jnp
from jax import lax
from jax.sharding import PartitionSpec as P

NE = 1024
HISTORY = 4
NREGION = 4
KMAX = 64
COLS = 64


def extended(block, sides, width):
    for axis, dim in sides:
        count = lax.axis_size(axis)
        forward = [(i, i + 1) for i in range(count - 1)]
        backward = [(target, source) for source, target in forward]
        low = lax.ppermute(
            lax.slice_in_dim(block, block.shape[dim] - width, None, axis=dim), axis, forward
        )
        high = lax.ppermute(lax.slice_in_dim(block, 0, width, axis=dim), axis, backward)
        block = jnp.concatenate([low, block, high], axis=dim)
    return block


def add_face(total, field, moved, mobility, moved_mob, valid):
    return total + jnp.where(valid, 0.5 * (mobility + moved_mob) * (moved - field), 0.0)


def local(dist, hist_x, hist_g, mobility, region, phonon_bins, coupling, hist_used):
    width = dist.shape[1]
    rows = dist.shape[2]
    cells = dist.shape[3]
    flat_g = hist_g.reshape(HISTORY, 2, -1)
    energy_ids = lax.axis_index("egrp") * width + jnp.arange(width, dtype=jnp.int32)
    dos = jnp.sqrt((energy_ids.astype(jnp.float32) + 0.5) / NE)
    even = dist[0]
    odd = dist[1]
    outrate = jnp.zeros(even.shape, jnp.float32)
    lam = jnp.zeros(region.shape, jnp.float32)
    for index in range(NREGION):
        offset = phonon_bins[index]
        lower = energy_ids - offset
        upper = energy_ids + offset
        dos_low = jnp.where(
            lower >= 0, jnp.sqrt((jnp.maximum(lower, 0).astype(jnp.float32) + 0.5) / NE), 0.0
        )
        dos_high = jnp.where(upper < NE, jnp.sqrt((upper.astype(jnp.float32) + 0.5) / NE), 0.0)
        rate = coupling[index] * (1.5 * dos_low + 0.5 * dos_high)
        outrate = jnp.where((region == index)[None], rate[:, None, None], outrate)
        lam = jnp.where(region == index, coupling[index], lam)
    column = lax.all_to_all(
        even.reshape(width, rows * cells), "egrp", split_axis=1, concat_axis=0, tiled=True
    )
    span = column.shape[1]
    column_region = lax.dynamic_slice_in_dim(
        region.reshape(-1), lax.axis_index("egrp") * span, span
    )
    padded = jnp.pad(column, ((KMAX, KMAX), (0, 0)))
    total = column.shape[0]
    partial_sum = jnp.zeros(column.shape, jnp.float32)
    for index in range(NREGION):
        offset = phonon_bins[index]
        above = lax.dynamic_slice_in_dim(padded, KMAX + offset, total, 0)
        below = lax.dynamic_slice_in_dim(padded, KMAX - offset, total, 0)
        partial_sum = jnp.where(
            (column_region == index)[None], 1.5 * above + 0.5 * below, partial_sum
        )
    shifted = lax.all_to_all(partial_sum, "egrp", split_axis=0, concat_axis=1, tiled=True).reshape(
        width, rows, cells
    )
    gain_in = lam[None] * dos[:, None, None] * shifted
    new_even = (even + gain_in) / (1.0 + outrate)
    new_odd = odd / (1.0 + outrate + lam[None])
    res = jnp.stack([new_even - even, new_odd - odd])
    res_flat = res.reshape(2, -1)
    cross = jnp.transpose(jnp.sum(flat_g.astype(jnp.float32) * res_flat[None], axis=2))
    self_term = jnp.sum(res_flat * res_flat, axis=1)
    among = lax.dot_general(
        flat_g, flat_g, (((2,), (2,)), ((1,), (1,))), preferred_element_type=jnp.float32
    )
    among, cross, self_term = lax.psum((among, cross, self_term), ("egrp", "space"))
    fields = []
    for field in range(2):
        top = jnp.concatenate([self_term[field][None], cross[field]])[None, :]
        lower_rows = jnp.concatenate([cross[field][:, None], among[field]], axis=1)
        gram = jnp.concatenate([top, lower_rows], axis=0)
        valid = jnp.concatenate([jnp.ones((1,), jnp.float32), hist_used[field].astype(jnp.float32)])
        masked = valid[:, None] * valid[None, :] * gram + jnp.diag(1.0 - valid) * gram[0, 0]
        factor = jnp.linalg.cholesky(masked)
        weights = jax.scipy.linalg.cho_solve((factor, True), valid)
        coeffs = weights / jnp.sum(weights)
        part_mix = coeffs[0] * (dist[field] + 0.5 * res[field])
        for index in range(HISTORY):
            part_mix = part_mix + coeffs[index + 1] * (
                hist_x[index, field].astype(jnp.float32)
                + 0.5 * hist_g[index, field].astype(jnp.float32)
            )
        fields.append(part_mix)
    mixed = jnp.stack(fields)
    mob_block = mobility[None, None]
    wide_field, wide_mob = (
        extended(mixed, (("space", 2),), 1),
        extended(mob_block, (("space", 2),), 1),
    )
    row_ids = lax.axis_index("space") * rows + jnp.arange(rows, dtype=jnp.int32)
    all_rows = lax.axis_size("space") * rows
    cell_ids = jnp.arange(cells, dtype=jnp.int32)
    column_ids = cell_ids % COLS
    lap = jnp.zeros(mixed.shape, jnp.float32)
    lap = add_face(
        lap,
        mixed,
        wide_field[:, :, 0:rows],
        mob_block,
        wide_mob[:, :, 0:rows],
        (row_ids > 0)[:, None],
    )
    lap = add_face(
        lap,
        mixed,
        wide_field[:, :, 2 : rows + 2],
        mob_block,
        wide_mob[:, :, 2 : rows + 2],
        (row_ids < all_rows - 1)[:, None],
    )
    for shift_by, valid_cells in (
        (1, column_ids > 0),
        (-1, column_ids < COLS - 1),
        (COLS, cell_ids >= COLS),
        (-COLS, cell_ids < COLS),
    ):
        moved = jnp.roll(mixed, shift_by, axis=3)
        moved_mob = jnp.roll(mob_block, shift_by, axis=3)
        lap = add_face(lap, mixed, moved, mob_block, moved_mob, valid_cells)
    drive = 0.25 * dos[:, None, None]
    out_even = mixed[0] + 0.08 * lap[0] + drive * mixed[1]
    out_odd = mixed[1] + 0.08 * lap[1] - drive * mixed[0]
    return jnp.stack([out_even, out_odd])


def solution(mesh):
    in_specs = (
        P(None, "egrp", "space", None),
        P(None, None, "egrp", "space", None),
        P(None, None, "egrp", "space", None),
        P("space", None),
        P("space", None),
        P(),
        P(),
        P(),
    )
    out_specs = P(None, "egrp", "space", None)
    return jax.shard_map(local, mesh=mesh, in_specs=in_specs, out_specs=out_specs, check_vma=False)
```

profile of v0, /device:TPU:11, one launch (start us, length us, event | category | flops | bytes accessed | tf_op | source)
XLA Modules:
  0.0 195.8 jit_solution(16239742261708099260)
XLA Ops:
  0.0 1.7 fusion.84
  1.7 1.4 copy.175
  3.1 3.8 %all-to-all-start = ((f32[512,2,256]{0,2,1:T(8,128)}), f32[512,2,256]{0,2,1:T(8,128)S(1)}, u32[]{:S(2)}, u32[]{:S(2)}) async-start(f32[512,2,256]{0,2,1:T(8,128)} %bitcast.6), calls=%async_computation | async-start | bytes 2097152 | tf_op jit(solution)/shard_map/all_to_all | solution.py:52
  6.9 4.0 %collective-permute-start = (f32[1,1,1,128]{3,2,1,0:T(1,128)S(1)}, f32[1,1,1,128]{3,2,1,0:T(1,128)S(1)}, u32[]{:S(2)}, u32[]{:S(2)}) collective-permute-start(f32[1,1,1,128]{3,2,1,0:T(1,128)S(1)} %get-tuple-element.53), channel_id=1, source_target_pairs={{0,1},{1,2},{2,3},{3,4},{4,5},{5,6},{6,7},{7,8},{8,9},{9,10},{10,1... | collective-permute-start | bytes 1544 | tf_op jit(solution)/shard_map/ppermute | solution.py:18
  10.9 1.9 collective-permute-start.2
  23.6 5.1 %reshape.555 = bf16[4,2,262144]{2,1,0:T(2,128)(2,1)} reshape(bf16[4,2,512,4,128]{4,3,2,1,0:T(4,128)(2,1)} %param.13) | data formatting | bytes 8388608 | tf_op jit(solution)/shard_map/reshape | solution.py:34
  28.7 4.1 %fusion.83 = (bf16[1,1,512,4,128]{4,3,2,1,0:T(4,128)(2,1)}, bf16[1,1,512,4,128]{4,3,2,1,0:T(4,128)(2,1)}, bf16[1,1,512,4,128]{4,3,2,1,0:T(4,128)(2,1)}, bf16[1,1...) fusion(bf16[4,2,512,4,128]{4,3,2,1,0:T(4,128)(2,1)} %param.13), kind=kLoop, calls=%fused_computation.196 | loop fusion | bytes 8388608 | tf_op jit(solution)/shard_map/slice | solution.py:97
  33.7 2.5 %add_multiply_fusion.2 = (f32[512]{0:T(512)S(1)}, f32[512]{0:T(512)S(1)}) fusion(s32[]{:T(128)} %bitcast.10, f32[]{:T(128)} %bitcast.2, s32[]{:T(128)S(6)} %mul.605, s32[]{:T(128)} %bitcast.9, f32[]{:T(128)} %bitcast.1), kind=kLoop, calls=%fused_computation.143 | loop fusion | flops 17920 | bytes 4116 | tf_op jit(solution)/shard_map/mul | solution.py:49
  36.2 2.5 %add_multiply_fusion = (f32[512]{0:T(512)S(1)}, f32[512]{0:T(512)S(1)}) fusion(s32[]{:T(128)} %bitcast.12, f32[]{:T(128)} %bitcast.4, s32[]{:T(128)S(6)} %mul.605, s32[]{:T(128)} %bitcast.11, f32[]{:T(128)} %bitcast.3), kind=kLoop, calls=%fused_computation.141 | loop fusion | flops 17920 | bytes 4116 | tf_op jit(solution)/shard_map/mul | solution.py:49
  38.7 2.4 %select_select_fusion.2 = (f32[4,128]{1,0:T(4,128)S(1)}, pred[4,128]{1,0:T(4,128)(4,1)S(1)}, pred[4,128]{1,0:T(4,128)(4,1)S(1)}, pred[4,128]{1,0:T(4,128)(4,1)S(1)}, pred[4,128]{1,0:T(4,128)(4,1)S(1)}) fusion(f32[]{:T(128)} %bitcast.4, f32[]{:T(128)} %bitcast.3, f32[]{:T(128)} %bitcast.2, f32[]{:T(128)} %bitcast.1, s32[4,128]{1,0:T(4,128)S(1)} %copy-done.22), kind=kLoop, calls=%fused_computation.163 | loop fusion | flops 4096 | bytes 6160 | tf_op jit(solution)/shard_map/jit(_where)/select_n | solution.py:51
  41.5 4.1 %fusion.82 = (bf16[1,1,512,4,128]{4,3,2,1,0:T(4,128)(2,1)}, bf16[1,1,512,4,128]{4,3,2,1,0:T(4,128)(2,1)}, bf16[1,1,512,4,128]{4,3,2,1,0:T(4,128)(2,1)}, bf16[1,1...) fusion(bf16[4,2,512,4,128]{4,3,2,1,0:T(4,128)(2,1)} %param.12), kind=kLoop, calls=%fused_computation.195 | loop fusion | bytes 8388608 | tf_op jit(solution)/shard_map/slice | solution.py:96
  45.7 2.2 %copy.185 = bf16[1,1,512,4,128]{2,4,3,1,0:T(8,128)(2,1)} copy(bf16[1,1,512,4,128]{4,3,2,1,0:T(4,128)(2,1)} %get-tuple-element.22) | data formatting | bytes 1048576
  47.9 1.1 copy.186
  49.0 2.1 %copy.187 = bf16[1,1,512,4,128]{2,4,3,1,0:T(8,128)(2,1)} copy(bf16[1,1,512,4,128]{4,3,2,1,0:T(4,128)(2,1)} %get-tuple-element.21) | data formatting | bytes 1048576
  51.1 1.1 copy.188
  52.2 2.2 %copy.189 = bf16[1,1,512,4,128]{2,4,3,1,0:T(8,128)(2,1)} copy(bf16[1,1,512,4,128]{4,3,2,1,0:T(4,128)(2,1)} %get-tuple-element.20) | data formatting | bytes 1048576
  54.4 2.2 %copy.190 = bf16[1,1,512,4,128]{2,4,3,1,0:T(8,128)(2,1)} copy(bf16[1,1,512,4,128]{4,3,2,1,0:T(4,128)(2,1)} %get-tuple-element.28) | data formatting | bytes 1048576
  56.6 2.1 %copy.191 = bf16[1,1,512,4,128]{2,4,3,1,0:T(8,128)(2,1)} copy(bf16[1,1,512,4,128]{4,3,2,1,0:T(4,128)(2,1)} %get-tuple-element.26) | data formatting | bytes 1048576
  58.7 1.2 copy.192
  59.8 2.2 %copy.177 = bf16[1,1,512,4,128]{2,4,3,1,0:T(8,128)(2,1)} copy(bf16[1,1,512,4,128]{4,3,2,1,0:T(4,128)(2,1)} %get-tuple-element.19) | data formatting | bytes 1048576
  62.0 1.2 copy.178
  63.2 1.1 copy.179
  65.0 2.3 %fusion.25 = f32[1024,256]{1,0:T(8,128)} fusion(s32[]{:T(128)S(6)} %select_n.228, f32[1024,256]{1,0:T(8,128)S(1)} %bitcast.141, s32[]{:T(128)S(6)} %select_n.229, s32[]{:T(128)S(6)} %select_n.230, s32[]{:T(128)S(6)} %select_n.231, s32[]{:T(128)S(6)} %select_n.232, s32[]{:T(128)S(6)} %select_n.233, s32[]{:T(128)S(6)} %select_n.234, s32[]{:T(128)S(6)} %select_n.235, ...), kind=kLoop, calls=%fused_computation.64 | loop fusion | flops 4194304 | bytes 2098208 | tf_op jit(solution)/shard_map/jit(_where)/select_n | solution.py:66
  67.3 3.8 %all-to-all-start.1 = ((f32[2,512,256]{2,1,0:T(8,128)}), f32[2,512,256]{2,1,0:T(8,128)S(1)}, u32[]{:S(2)}, u32[]{:S(2)}) async-start(f32[2,512,256]{2,1,0:T(8,128)} %bitcast.13), calls=%async_computation.1 | async-start | bytes 2097152 | tf_op jit(solution)/shard_map/all_to_all | solution.py:69
  71.1 9.5 %fusion = f32[2,4,4]{2,1,0:T(4,128)S(1)} fusion(bf16[4,2,262144]{2,1,0:T(2,128)(2,1)} %reshape.555), kind=kOutput, calls=%fused_computation.18 | convolution fusion | flops 16777216 | bytes 4194432 | tf_op jit(solution)/shard_map/dot_general | solution.py:79
  80.6 2.2 %copy.180 = bf16[1,1,512,4,128]{2,4,3,1,0:T(8,128)(2,1)} copy(bf16[1,1,512,4,128]{4,3,2,1,0:T(4,128)(2,1)} %get-tuple-element.33) | data formatting | bytes 1048576
  82.8 2.1 %copy.181 = bf16[1,1,512,4,128]{2,4,3,1,0:T(8,128)(2,1)} copy(bf16[1,1,512,4,128]{4,3,2,1,0:T(4,128)(2,1)} %get-tuple-element.24) | data formatting | bytes 1048576
  84.9 1.1 copy.182
  86.0 2.1 %copy.183 = bf16[1,1,512,4,128]{2,4,3,1,0:T(8,128)(2,1)} copy(bf16[1,1,512,4,128]{4,3,2,1,0:T(4,128)(2,1)} %get-tuple-element.23) | data formatting | bytes 1048576
  88.1 1.1 copy.184
  89.3 1.3 copy.141
  90.6 2.3 %divide_subtract_fusion.1 = (f32[1,512,4,128]{1,3,2,0:T(8,128)S(1)}, f32[1,512,4,128]{1,3,2,0:T(8,128)S(1)}) fusion(f32[1,512,4,128]{1,3,2,0:T(8,128)} %copy.175, f32[1,512,4,128]{1,3,2,0:T(8,128)} %bitcast.146, f32[512]{0:T(512)S(1)} %get-tuple-element.98, f32[512]{0:T(512)S(1)} %get-tuple-element.99, f32[512]{0:T(512)S(1)} %get-tuple-element.100, ...), kind=kLoop, calls=%fused_computation.94 | loop fusion | flops 3407872 | bytes 5257216 | tf_op jit(solution)/shard_map/sub | solution.py:75
  92.9 1.3 copy.142
  94.2 1.3 copy.144
  95.6 1.6 pad_maximum_fusion.5
  97.2 2.9 %copy.145 = f32[2,512,4,128]{3,2,1,0:T(4,128)} copy(f32[2,512,4,128]{1,3,2,0:T(8,128)} %pad_maximum_fusion.5) | data formatting | bytes 4194304 | tf_op jit(solution)/shard_map/stack | solution.py:75
  100.1 5.3 %multiply_reduce_fusion = f32[4,2]{1,0:T(4,128)S(1)} fusion(bf16[4,2,512,4,128]{4,3,2,1,0:T(4,128)(2,1)} %param.13, f32[2,512,4,128]{3,2,1,0:T(4,128)} %copy.145), kind=kLoop, calls=%fused_computation | loop fusion | flops 6291448 | bytes 6291488 | tf_op jit(solution)/shard_map/reduce_sum | solution.py:77
  105.4 2.3 %fusion.15 = f32[2]{0:T(128)S(1)} fusion(f32[1,262144]{1,0:T(1,128)S(1)} %bitcast.143, f32[1,262144]{1,0:T(1,128)S(1)} %bitcast.142), kind=kLoop, calls=%fused_computation.38 | loop fusion | flops 1572862 | bytes 2097160 | tf_op jit(solution)/shard_map/reduce_sum | solution.py:78
  107.7 40.7 %all-reduce.1 = (f32[2,4,4]{2,1,0:T(4,128)S(1)}, f32[2,4]{0,1:T(4,128)S(1)}, f32[2]{0:T(128)S(1)}) all-reduce(f32[2,4,4]{2,1,0:T(4,128)S(1)} %fusion, f32[2,4]{0,1:T(4,128)S(1)} %bitcast.152, f32[2]{0:T(128)S(1)} %fusion.15), channel_id=1, replica_groups=mesh['egrp'=2,'space'=16] {'egrp','space'}, use_global_device_ids=true, to_apply=%region_4.5 | all-reduce | flops 42 | bytes 336 | tf_op jit(solution)/shard_map/psum | solution.py:82
  152.8 0.8 fusion.92
  160.6 6.4 %bitcast_add_fusion = f32[1,512,4,128]{1,3,2,0:T(8,128)S(1)} fusion(bf16[1,1,512,4,128]{2,4,3,1,0:T(8,128)(2,1)} %copy.192, bf16[1,1,512,4,128]{2,4,3,1,0:T(8,128)(2,1)} %copy.191, bf16[1,1,512,4,128]{2,4,3,1,0:T(8,128)(2,1)} %copy.190, bf16[1,1,512,4,128]{2,4,3,1,0:T(8,128)(2,1)} %copy.189, bf16[1,1,512,4,128]{2,4,3,1,0:T(8,128)(2,1)} %copy.188, ...), kind=kLoop, calls=%fused_computation.86 | loop fusion | flops 9175040 | bytes 6303764 | tf_op jit(solution)/shard_map/add | solution.py:95
  167.1 5.4 %bitcast_add_fusion.4 = f32[1,512,4,128]{1,3,2,0:T(8,128)S(1)} fusion(bf16[1,1,512,4,128]{2,4,3,1,0:T(8,128)(2,1)S(1)} %copy-done.18, bf16[1,1,512,4,128]{2,4,3,1,0:T(8,128)(2,1)S(1)} %copy-done.17, bf16[1,1,512,4,128]{2,4,3,1,0:T(8,128)(2,1)S(1)} %copy-done.16, bf16[1,1,512,4,128]{2,4,3,1,0:T(8,128)(2,1)S(1)} %copy-done.15, ...), kind=kLoop, calls=%fused_computation.90 | loop fusion | flops 7077888 | bytes 7340052 | tf_op jit(solution)/shard_map/add | solution.py:95
  172.5 4.5 %collective-permute-start.1 = (f32[2,512,1,128]{1,3,2,0:T(8,128)S(1)}, f32[2,512,1,128]{1,3,2,0:T(8,128)S(1)}, u32[]{:S(2)}, u32[]{:S(2)}) collective-permute-start(f32[2,512,1,128]{1,3,2,0:T(8,128)S(1)} %get-tuple-element.41), channel_id=1, source_target_pairs={{0,1},{1,2},{2,3},{3,4},{4,5},{5,6},{6,7},{7,8},{8,9},{9,10},{10,1... | collective-permute-start | bytes 1572872 | tf_op jit(solution)/shard_map/ppermute | solution.py:18
  177.0 1.9 collective-permute-start.3
  179.7 9.0 %collective-permute-done.1 = f32[2,512,1,128]{1,3,2,0:T(8,128)S(1)} collective-permute-done((f32[2,512,1,128]{1,3,2,0:T(8,128)S(1)}, f32[2,512,1,128]{1,3,2,0:T(8,128)S(1)}, u32[]{:S(2)}, u32[]{:S(2)}) %collective-permute-start.1) | collective-permute-done | bytes 524320 | tf_op jit(solution)/shard_map/ppermute | solution.py:18
  188.7 1.6 collective-permute-done.3
  190.3 2.9 %fusion.11 = f32[2,512,4,128]{1,3,2,0:T(8,128)S(1)} fusion(f32[2,512,1,128]{1,3,2,0:T(8,128)S(1)} %collective-permute-done.3, f32[1,512,4,128]{1,3,2,0:T(8,128)S(1)} %bitcast_add_fusion, f32[1,512,4,128]{1,3,2,0:T(8,128)S(1)} %bitcast_add_fusion.4, f32[2,512,1,128]{1,3,2,0:T(8,128)S(1)} %collective-permute-done.1, ...), kind=kLoop, calls=%fused_computation.30 | loop fusion | flops 15204352 | bytes 11545096 | tf_op jit(solution)/shard_map/add | solution.py:27
  194.0 1.8 copy.174
  (109 shorter events, 15.5 us)
Async XLA Ops:
  1.7 5.3 %copy-start.19 = (f32[4,128]{1,0:T(4,128)S(1)}, f32[4,128]{1,0:T(4,128)}, u32[]{:S(2)}) copy-start(f32[4,128]{1,0:T(4,128)} %param.14) | copy-start | bytes 6148
  1.7 11.2 %copy-start.20 = (s32[4]{0:T(128)S(1)}, s32[4]{0:T(128)}, u32[]{:S(2)}) copy-start(s32[4]{0:T(128)} %param.16) | copy-start | bytes 52
  3.1 61.6 %all-to-all-start = ((f32[512,2,256]{0,2,1:T(8,128)}), f32[512,2,256]{0,2,1:T(8,128)S(1)}, u32[]{:S(2)}, u32[]{:S(2)}) async-start(f32[512,2,256]{0,2,1:T(8,128)} %bitcast.6), calls=%async_computation | async-start | bytes 2097152 | tf_op jit(solution)/shard_map/all_to_all | solution.py:52
  6.9 82.3 %collective-permute-start = (f32[1,1,1,128]{3,2,1,0:T(1,128)S(1)}, f32[1,1,1,128]{3,2,1,0:T(1,128)S(1)}, u32[]{:S(2)}, u32[]{:S(2)}) collective-permute-start(f32[1,1,1,128]{3,2,1,0:T(1,128)S(1)} %get-tuple-element.53), channel_id=1, source_target_pairs={{0,1},{1,2},{2,3},{3,4},{4,5},{5,6},{6,7},{7,8},{8,9},{9,10},{10,1... | collective-permute-start | bytes 1544 | tf_op jit(solution)/shard_map/ppermute | solution.py:18
  10.9 78.3 %collective-permute-start.2 = (f32[1,1,1,128]{3,2,1,0:T(1,128)S(1)}, f32[1,1,1,128]{3,2,1,0:T(1,128)S(1)}, u32[]{:S(2)}, u32[]{:S(2)}) collective-permute-start(f32[1,1,1,128]{3,2,1,0:T(1,128)S(1)} %get-tuple-element.54), channel_id=1, source_target_pairs={{1,0},{2,1},{3,2},{4,3},{5,4},{6,5},{7,6},{8,7},{9,8},{10,9},{11,1... | collective-permute-start | bytes 1544 | tf_op jit(solution)/shard_map/ppermute | solution.py:21
  28.7 4.3 %copy-start.21 = (f32[4]{0:T(128)S(1)}, f32[4]{0:T(128)}, u32[]{:S(2)}) copy-start(f32[4]{0:T(128)} %param.17) | copy-start | bytes 52
  28.7 10.0 %copy-start.22 = (s32[4,128]{1,0:T(4,128)S(1)}, s32[4,128]{1,0:T(4,128)}, u32[]{:S(2)}) copy-start(s32[4,128]{1,0:T(4,128)} %param.15) | copy-start | bytes 6148
  32.8 8.7 %copy-start.23 = (s32[2,4]{1,0:T(2,128)S(1)}, s32[2,4]{1,0:T(2,128)}, u32[]{:S(2)}) copy-start(s32[2,4]{1,0:T(2,128)} %param.18) | copy-start | bytes 100
  41.5 6.3 %copy-start.7 = (bf16[1,1,512,4,128]{4,3,2,1,0:T(4,128)(2,1)S(1)}, bf16[1,1,512,4,128]{4,3,2,1,0:T(4,128)(2,1)}, u32[]{:S(2)}) copy-start(bf16[1,1,512,4,128]{4,3,2,1,0:T(4,128)(2,1)} %get-tuple-element.30) | copy-start | bytes 1572868
  45.7 5.4 %copy-start.6 = (bf16[1,1,512,4,128]{4,3,2,1,0:T(4,128)(2,1)S(1)}, bf16[1,1,512,4,128]{4,3,2,1,0:T(4,128)(2,1)}, u32[]{:S(2)}) copy-start(bf16[1,1,512,4,128]{4,3,2,1,0:T(4,128)(2,1)} %get-tuple-element.29) | copy-start | bytes 1572868
  51.1 7.6 %copy-start.5 = (bf16[1,1,512,4,128]{4,3,2,1,0:T(4,128)(2,1)S(1)}, bf16[1,1,512,4,128]{4,3,2,1,0:T(4,128)(2,1)}, u32[]{:S(2)}) copy-start(bf16[1,1,512,4,128]{4,3,2,1,0:T(4,128)(2,1)} %get-tuple-element.34) | copy-start | bytes 1572868
  54.4 7.7 %copy-start.4 = (bf16[1,1,512,4,128]{4,3,2,1,0:T(4,128)(2,1)S(1)}, bf16[1,1,512,4,128]{4,3,2,1,0:T(4,128)(2,1)}, u32[]{:S(2)}) copy-start(bf16[1,1,512,4,128]{4,3,2,1,0:T(4,128)(2,1)} %get-tuple-element.27) | copy-start | bytes 1572868
  59.8 3.4 %copy-start.8 = (bf16[1,1,512,4,128]{4,3,2,1,0:T(4,128)(2,1)S(1)}, bf16[1,1,512,4,128]{4,3,2,1,0:T(4,128)(2,1)}, u32[]{:S(2)}) copy-start(bf16[1,1,512,4,128]{4,3,2,1,0:T(4,128)(2,1)} %get-tuple-element.25) | copy-start | bytes 1572868
  67.3 22.0 %all-to-all-start.1 = ((f32[2,512,256]{2,1,0:T(8,128)}), f32[2,512,256]{2,1,0:T(8,128)S(1)}, u32[]{:S(2)}, u32[]{:S(2)}) async-start(f32[2,512,256]{2,1,0:T(8,128)} %bitcast.13), calls=%async_computation.1 | async-start | bytes 2097152 | tf_op jit(solution)/shard_map/all_to_all | solution.py:69
  80.6 4.3 %copy-start.3 = (bf16[1,1,512,4,128]{4,3,2,1,0:T(4,128)(2,1)S(1)}, bf16[1,1,512,4,128]{4,3,2,1,0:T(4,128)(2,1)}, u32[]{:S(2)}) copy-start(bf16[1,1,512,4,128]{4,3,2,1,0:T(4,128)(2,1)} %get-tuple-element.32) | copy-start | bytes 1572868
  80.6 7.5 %copy-start.2 = (bf16[1,1,512,4,128]{4,3,2,1,0:T(4,128)(2,1)S(1)}, bf16[1,1,512,4,128]{4,3,2,1,0:T(4,128)(2,1)}, u32[]{:S(2)}) copy-start(bf16[1,1,512,4,128]{4,3,2,1,0:T(4,128)(2,1)} %get-tuple-element.31) | copy-start | bytes 1572868
  100.1 5.3 %copy-start = (f32[1,512,4,128]{3,2,1,0:T(4,128)S(1)}, f32[1,512,4,128]{3,2,1,0:T(4,128)}, u32[]{:S(2)}) copy-start(f32[1,512,4,128]{3,2,1,0:T(4,128)} %copy.142) | copy-start | bytes 3145732
  100.1 5.3 %copy-start.1 = (f32[1,512,4,128]{3,2,1,0:T(4,128)S(1)}, f32[1,512,4,128]{3,2,1,0:T(4,128)}, u32[]{:S(2)}) copy-start(f32[1,512,4,128]{3,2,1,0:T(4,128)} %copy.144) | copy-start | bytes 3145732
  105.4 55.1 %copy-start.9 = (bf16[1,1,512,4,128]{2,4,3,1,0:T(8,128)(2,1)S(1)}, bf16[1,1,512,4,128]{2,4,3,1,0:T(8,128)(2,1)}, u32[]{:S(2)}) copy-start(bf16[1,1,512,4,128]{2,4,3,1,0:T(8,128)(2,1)} %copy.185) | copy-start | bytes 1572868
  105.4 55.1 %copy-start.11 = (bf16[1,1,512,4,128]{2,4,3,1,0:T(8,128)(2,1)S(1)}, bf16[1,1,512,4,128]{2,4,3,1,0:T(8,128)(2,1)}, u32[]{:S(2)}) copy-start(bf16[1,1,512,4,128]{2,4,3,1,0:T(8,128)(2,1)} %copy.186) | copy-start | bytes 1572868
  160.6 6.4 %copy-start.10 = (bf16[1,1,512,4,128]{2,4,3,1,0:T(8,128)(2,1)S(1)}, bf16[1,1,512,4,128]{2,4,3,1,0:T(8,128)(2,1)}, u32[]{:S(2)}) copy-start(bf16[1,1,512,4,128]{2,4,3,1,0:T(8,128)(2,1)} %copy.177) | copy-start | bytes 1572868
  160.6 6.4 %copy-start.12 = (bf16[1,1,512,4,128]{2,4,3,1,0:T(8,128)(2,1)S(1)}, bf16[1,1,512,4,128]{2,4,3,1,0:T(8,128)(2,1)}, u32[]{:S(2)}) copy-start(bf16[1,1,512,4,128]{2,4,3,1,0:T(8,128)(2,1)} %copy.178) | copy-start | bytes 1572868
  160.6 6.4 %copy-start.13 = (bf16[1,1,512,4,128]{2,4,3,1,0:T(8,128)(2,1)S(1)}, bf16[1,1,512,4,128]{2,4,3,1,0:T(8,128)(2,1)}, u32[]{:S(2)}) copy-start(bf16[1,1,512,4,128]{2,4,3,1,0:T(8,128)(2,1)} %copy.179) | copy-start | bytes 1572868
  160.6 6.4 %copy-start.14 = (bf16[1,1,512,4,128]{2,4,3,1,0:T(8,128)(2,1)S(1)}, bf16[1,1,512,4,128]{2,4,3,1,0:T(8,128)(2,1)}, u32[]{:S(2)}) copy-start(bf16[1,1,512,4,128]{2,4,3,1,0:T(8,128)(2,1)} %copy.180) | copy-start | bytes 1572868
  160.6 6.4 %copy-start.15 = (bf16[1,1,512,4,128]{2,4,3,1,0:T(8,128)(2,1)S(1)}, bf16[1,1,512,4,128]{2,4,3,1,0:T(8,128)(2,1)}, u32[]{:S(2)}) copy-start(bf16[1,1,512,4,128]{2,4,3,1,0:T(8,128)(2,1)} %copy.181) | copy-start | bytes 1572868
  160.6 6.4 %copy-start.16 = (bf16[1,1,512,4,128]{2,4,3,1,0:T(8,128)(2,1)S(1)}, bf16[1,1,512,4,128]{2,4,3,1,0:T(8,128)(2,1)}, u32[]{:S(2)}) copy-start(bf16[1,1,512,4,128]{2,4,3,1,0:T(8,128)(2,1)} %copy.182) | copy-start | bytes 1572868
  160.6 6.4 %copy-start.17 = (bf16[1,1,512,4,128]{2,4,3,1,0:T(8,128)(2,1)S(1)}, bf16[1,1,512,4,128]{2,4,3,1,0:T(8,128)(2,1)}, u32[]{:S(2)}) copy-start(bf16[1,1,512,4,128]{2,4,3,1,0:T(8,128)(2,1)} %copy.183) | copy-start | bytes 1572868
  160.6 6.4 %copy-start.18 = (bf16[1,1,512,4,128]{2,4,3,1,0:T(8,128)(2,1)S(1)}, bf16[1,1,512,4,128]{2,4,3,1,0:T(8,128)(2,1)}, u32[]{:S(2)}) copy-start(bf16[1,1,512,4,128]{2,4,3,1,0:T(8,128)(2,1)} %copy.184) | copy-start | bytes 1572868
  172.5 16.2 %collective-permute-start.1 = (f32[2,512,1,128]{1,3,2,0:T(8,128)S(1)}, f32[2,512,1,128]{1,3,2,0:T(8,128)S(1)}, u32[]{:S(2)}, u32[]{:S(2)}) collective-permute-start(f32[2,512,1,128]{1,3,2,0:T(8,128)S(1)} %get-tuple-element.41), channel_id=1, source_target_pairs={{0,1},{1,2},{2,3},{3,4},{4,5},{5,6},{6,7},{7,8},{8,9},{9,10},{10,1... | collective-permute-start | bytes 1572872 | tf_op jit(solution)/shard_map/ppermute | solution.py:18
  177.0 13.3 %collective-permute-start.3 = (f32[2,512,1,128]{1,3,2,0:T(8,128)S(1)}, f32[2,512,1,128]{1,3,2,0:T(8,128)S(1)}, u32[]{:S(2)}, u32[]{:S(2)}) collective-permute-start(f32[2,512,1,128]{1,3,2,0:T(8,128)S(1)} %get-tuple-element.42), channel_id=1, source_target_pairs={{1,0},{2,1},{3,2},{4,3},{5,4},{6,5},{7,6},{8,7},{9,8},{10,9},{11,1... | collective-permute-start | bytes 1572872 | tf_op jit(solution)/shard_map/ppermute | solution.py:21
where the time goes:
time: 197 us; the launch traced here: 196 us
  local copies, waits for them, and re-layouts  57.4 us (29%)
  other arithmetic  45.2 us (23%)
  blocking collectives  40.7 us (21%)
  starting transfers between devices  19.9 us (10%)
  matrix products  11.5 us (6%)
  waiting for transfers between devices  10.6 us (5%)
  between operations  10.6 us (5%)
    psum x1, blocking collectives, local(): lax.psum((among, cross, self_term), ('egrp', 'space'))  40.7 us
    unnamed x66, local copies, waits for them, and re-layouts  29.2 us
    add x2, other arithmetic, local(): part_mix + coeffs[index + 1] * (hist_x[index, field].astype(jnp.float32)...  11.7 us
    dot_general x1, matrix products, local(): lax.dot_general(flat_g, flat_g, (((2,), (2,)), ((1,), (1,))), preferred_e...  9.54 us
    ppermute x2, waiting for transfers between devices, extended(): lax.ppermute(lax.slice_in_dim(block, block.shape[dim] - width, None, axis...  9 us
    ppermute x2, starting transfers between devices, extended(): lax.ppermute(lax.slice_in_dim(block, block.shape[dim] - width, None, axis...  8.46 us
    reduce_sum x1, other arithmetic, local(): jnp.sum(flat_g.astype(jnp.float32) * res_flat[None], axis=2)  5.32 us
    reshape x1, local copies, waits for them, and re-layouts, local(): flat_g = hist_g.reshape(HISTORY, 2, -1)  5.11 us
  transfers between devices with their start and end apart: 6, of which 2 were waited for; matrix products, arithmetic and copies ran while one was open for 32% of the time, Pallas kernels for 0%

commit v1 on v0

--- a/solution.py
+++ b/solution.py
@@ -49,8 +49,14 @@
         rate = coupling[index] * (1.5 * dos_low + 0.5 * dos_high)
         outrate = jnp.where((region == index)[None], rate[:, None, None], outrate)
         lam = jnp.where(region == index, coupling[index], lam)
-    column = lax.all_to_all(
-        even.reshape(width, rows * cells), "egrp", split_axis=1, concat_axis=0, tiled=True
+    column = jnp.concatenate(
+        lax.all_to_all(
+            jnp.stack(jnp.split(even.reshape(width, rows * cells), lax.axis_size("egrp"), axis=1)),
+            "egrp",
+            0,
+            0,
+        ),
+        axis=0,
     )
     span = column.shape[1]
     column_region = lax.dynamic_slice_in_dim(

time: 197 us -> 209 us (1.061)
  local copies, waits for them, and re-layouts: 57.4 us -> 66.7 us
    unnamed x66 -> x50, local copies, waits for them, and re-layouts: 29.2 us -> 36.2 us
  transfers between devices with their start and end apart: 6 -> 6, of which waited for: 2 -> 2; matrix products, arithmetic and copies ran while one was open for 32% -> 34% of each run, Pallas kernels for 0% -> 0%
where the time goes in v1:
time: 209 us; the launch traced here: 207 us
  local copies, waits for them, and re-layouts  66.7 us (32%)
  other arithmetic  47.1 us (23%)
  blocking collectives  40.7 us (19%)
  starting transfers between devices  19.9 us (10%)
  matrix products  11.5 us (6%)
  between operations  11 us (5%)
  waiting for transfers between devices  10.6 us (5%)
    psum x1, blocking collectives, local(): lax.psum((among, cross, self_term), ('egrp', 'space'))  40.7 us
    unnamed x50, local copies, waits for them, and re-layouts  36.2 us
    add x2, other arithmetic, local(): part_mix + coeffs[index + 1] * (hist_x[index, field].astype(jnp.float32)...  10.6 us
    dot_general x1, matrix products, local(): lax.dot_general(flat_g, flat_g, (((2,), (2,)), ((1,), (1,))), preferred_e...  9.54 us
    ppermute x2, waiting for transfers between devices, extended(): lax.ppermute(lax.slice_in_dim(block, block.shape[dim] - width, None, axis...  9 us
    ppermute x2, starting transfers between devices, extended(): lax.ppermute(lax.slice_in_dim(block, block.shape[dim] - width, None, axis...  8.46 us
    reduce_sum x1, other arithmetic, local(): jnp.sum(flat_g.astype(jnp.float32) * res_flat[None], axis=2)  5.32 us
    reshape x1, local copies, waits for them, and re-layouts, local(): flat_g = hist_g.reshape(HISTORY, 2, -1)  5.17 us
  transfers between devices with their start and end apart: 6, of which 2 were waited for; matrix products, arithmetic and copies ran while one was open for 34% of the time, Pallas kernels for 0%

profile of v1, /device:TPU:11, one launch (start us, length us, event | category | flops | bytes accessed | tf_op | source)
XLA Modules:
  0.0 207.4 jit_solution(7190393212575416732)
XLA Ops:
  0.0 2.6 %fusion.84 = (f32[1,512,4,128]{3,2,1,0:T(4,128)S(1)}, f32[1,512,4,128]{3,2,1,0:T(4,128)}) fusion(f32[2,512,4,128]{3,2,1,0:T(4,128)} %param.11), kind=kLoop, calls=%fused_computation.198 | loop fusion | bytes 4194304 | tf_op jit(solution)/shard_map/slice | solution.py:37
  3.5 1.0 pad_maximum_fusion.7
  4.6 3.8 %all-to-all-start = ((f32[2,512,256]{2,1,0:T(8,128)}), f32[2,512,256]{2,1,0:T(8,128)S(1)}, u32[]{:S(2)}, u32[]{:S(2)}) async-start(f32[2,512,256]{2,1,0:T(8,128)} %pad_maximum_fusion.7), calls=%async_computation | async-start | bytes 2097152 | tf_op jit(solution)/shard_map/all_to_all | solution.py:53
  8.4 4.0 %collective-permute-start = (f32[1,1,1,128]{3,2,1,0:T(1,128)S(1)}, f32[1,1,1,128]{3,2,1,0:T(1,128)S(1)}, u32[]{:S(2)}, u32[]{:S(2)}) collective-permute-start(f32[1,1,1,128]{3,2,1,0:T(1,128)S(1)} %get-tuple-element.55), channel_id=1, source_target_pairs={{0,1},{1,2},{2,3},{3,4},{4,5},{5,6},{6,7},{7,8},{8,9},{9,10},{10,1... | collective-permute-start | bytes 1544 | tf_op jit(solution)/shard_map/ppermute | solution.py:18
  12.4 1.9 collective-permute-start.2
  25.5 5.2 %reshape.555 = bf16[4,2,262144]{2,1,0:T(2,128)(2,1)} reshape(bf16[4,2,512,4,128]{4,3,2,1,0:T(4,128)(2,1)} %param.13) | data formatting | bytes 8388608 | tf_op jit(solution)/shard_map/reshape | solution.py:34
  30.6 4.2 %fusion.83 = (bf16[1,1,512,4,128]{4,3,2,1,0:T(4,128)(2,1)}, bf16[1,1,512,4,128]{4,3,2,1,0:T(4,128)(2,1)}, bf16[1,1,512,4,128]{4,3,2,1,0:T(4,128)(2,1)}, bf16[1,1...) fusion(bf16[4,2,512,4,128]{4,3,2,1,0:T(4,128)(2,1)} %param.13), kind=kLoop, calls=%fused_computation.197 | loop fusion | bytes 8388608 | tf_op jit(solution)/shard_map/slice | solution.py:103
  35.7 2.6 %add_multiply_fusion = (f32[512]{0:T(512)S(1)}, f32[512]{0:T(512)S(1)}) fusion(s32[]{:T(128)} %bitcast.13, f32[]{:T(128)} %bitcast.4, s32[]{:T(128)S(6)} %mul.605, s32[]{:T(128)} %bitcast.12, f32[]{:T(128)} %bitcast.3), kind=kLoop, calls=%fused_computation.142 | loop fusion | flops 17920 | bytes 4116 | tf_op jit(solution)/shard_map/mul | solution.py:49
  38.4 2.5 %add_multiply_fusion.2 = (f32[512]{0:T(512)S(1)}, f32[512]{0:T(512)S(1)}) fusion(s32[]{:T(128)} %bitcast.11, f32[]{:T(128)} %bitcast.2, s32[]{:T(128)S(6)} %mul.605, s32[]{:T(128)} %bitcast.10, f32[]{:T(128)} %bitcast.1), kind=kLoop, calls=%fused_computation.144 | loop fusion | flops 17920 | bytes 4116 | tf_op jit(solution)/shard_map/mul | solution.py:49
  40.9 2.5 %select_select_fusion.2 = (f32[4,128]{1,0:T(4,128)S(1)}, pred[4,128]{1,0:T(4,128)(4,1)S(1)}, pred[4,128]{1,0:T(4,128)(4,1)S(1)}, pred[4,128]{1,0:T(4,128)(4,1)S(1)}, pred[4,128]{1,0:T(4,128)(4,1)S(1)}) fusion(f32[]{:T(128)} %bitcast.4, f32[]{:T(128)} %bitcast.3, f32[]{:T(128)} %bitcast.2, f32[]{:T(128)} %bitcast.1, s32[4,128]{1,0:T(4,128)S(1)} %copy-done.13), kind=kLoop, calls=%fused_computation.164 | loop fusion | flops 4096 | bytes 6160 | tf_op jit(solution)/shard_map/jit(_where)/select_n | solution.py:51
  43.4 1.6 copy.182
  45.0 4.1 %fusion.82 = (bf16[1,1,512,4,128]{4,3,2,1,0:T(4,128)(2,1)}, bf16[1,1,512,4,128]{4,3,2,1,0:T(4,128)(2,1)}, bf16[1,1,512,4,128]{4,3,2,1,0:T(4,128)(2,1)}, bf16[1,1...) fusion(bf16[4,2,512,4,128]{4,3,2,1,0:T(4,128)(2,1)} %param.12), kind=kLoop, calls=%fused_computation.196 | loop fusion | bytes 8388608 | tf_op jit(solution)/shard_map/slice | solution.py:102
  49.0 2.1 %copy.191 = bf16[1,1,512,4,128]{2,4,3,1,0:T(8,128)(2,1)} copy(bf16[1,1,512,4,128]{4,3,2,1,0:T(4,128)(2,1)} %get-tuple-element.22) | data formatting | bytes 1048576
  51.1 2.1 %copy.192 = bf16[1,1,512,4,128]{2,4,3,1,0:T(8,128)(2,1)} copy(bf16[1,1,512,4,128]{4,3,2,1,0:T(4,128)(2,1)} %get-tuple-element.30) | data formatting | bytes 1048576
  53.2 2.1 %copy.193 = bf16[1,1,512,4,128]{2,4,3,1,0:T(8,128)(2,1)} copy(bf16[1,1,512,4,128]{4,3,2,1,0:T(4,128)(2,1)} %get-tuple-element.21) | data formatting | bytes 1048576
  55.4 2.1 %copy.194 = bf16[1,1,512,4,128]{2,4,3,1,0:T(8,128)(2,1)} copy(bf16[1,1,512,4,128]{4,3,2,1,0:T(4,128)(2,1)} %get-tuple-element.29) | data formatting | bytes 1048576
  57.5 2.1 %copy.195 = bf16[1,1,512,4,128]{2,4,3,1,0:T(8,128)(2,1)} copy(bf16[1,1,512,4,128]{4,3,2,1,0:T(4,128)(2,1)} %get-tuple-element.20) | data formatting | bytes 1048576
  59.6 2.1 %copy.196 = bf16[1,1,512,4,128]{2,4,3,1,0:T(8,128)(2,1)} copy(bf16[1,1,512,4,128]{4,3,2,1,0:T(4,128)(2,1)} %get-tuple-element.28) | data formatting | bytes 1048576
  61.7 2.1 %copy.197 = bf16[1,1,512,4,128]{2,4,3,1,0:T(8,128)(2,1)} copy(bf16[1,1,512,4,128]{4,3,2,1,0:T(4,128)(2,1)} %get-tuple-element.26) | data formatting | bytes 1048576
  63.8 2.1 %copy.198 = bf16[1,1,512,4,128]{2,4,3,1,0:T(8,128)(2,1)} copy(bf16[1,1,512,4,128]{4,3,2,1,0:T(4,128)(2,1)} %get-tuple-element.34) | data formatting | bytes 1048576
  65.9 2.1 %copy.183 = bf16[1,1,512,4,128]{2,4,3,1,0:T(8,128)(2,1)} copy(bf16[1,1,512,4,128]{4,3,2,1,0:T(4,128)(2,1)} %get-tuple-element.19) | data formatting | bytes 1048576
  68.0 2.1 %copy.184 = bf16[1,1,512,4,128]{2,4,3,1,0:T(8,128)(2,1)} copy(bf16[1,1,512,4,128]{4,3,2,1,0:T(4,128)(2,1)} %get-tuple-element.27) | data formatting | bytes 1048576
  70.2 2.1 %copy.185 = bf16[1,1,512,4,128]{2,4,3,1,0:T(8,128)(2,1)} copy(bf16[1,1,512,4,128]{4,3,2,1,0:T(4,128)(2,1)} %get-tuple-element.25) | data formatting | bytes 1048576
  72.6 2.3 %fusion.25 = f32[1024,256]{1,0:T(8,128)} fusion(s32[]{:T(128)S(6)} %select_n.228, f32[1024,256]{1,0:T(8,128)S(1)} %bitcast.143, s32[]{:T(128)S(6)} %select_n.229, s32[]{:T(128)S(6)} %select_n.230, s32[]{:T(128)S(6)} %select_n.231, s32[]{:T(128)S(6)} %select_n.232, s32[]{:T(128)S(6)} %select_n.233, s32[]{:T(128)S(6)} %select_n.234, s32[]{:T(128)S(6)} %select_n.235, ...), kind=kLoop, calls=%fused_computation.64 | loop fusion | flops 4194304 | bytes 2098208 | tf_op jit(solution)/shard_map/jit(_where)/select_n | solution.py:72
  74.8 3.8 %all-to-all-start.1 = ((f32[2,512,256]{2,1,0:T(8,128)}), f32[2,512,256]{2,1,0:T(8,128)S(1)}, u32[]{:S(2)}, u32[]{:S(2)}) async-start(f32[2,512,256]{2,1,0:T(8,128)} %bitcast.144), calls=%async_computation.1 | async-start | bytes 2097152 | tf_op jit(solution)/shard_map/all_to_all | solution.py:75
  78.6 9.5 %fusion = f32[2,4,4]{2,1,0:T(4,128)S(1)} fusion(bf16[4,2,262144]{2,1,0:T(2,128)(2,1)} %reshape.555), kind=kOutput, calls=%fused_computation.18 | convolution fusion | flops 16777216 | bytes 4194432 | tf_op jit(solution)/shard_map/dot_general | solution.py:85
  88.1 2.1 %copy.186 = bf16[1,1,512,4,128]{2,4,3,1,0:T(8,128)(2,1)} copy(bf16[1,1,512,4,128]{4,3,2,1,0:T(4,128)(2,1)} %get-tuple-element.33) | data formatting | bytes 1048576
  90.3 2.1 %copy.187 = bf16[1,1,512,4,128]{2,4,3,1,0:T(8,128)(2,1)} copy(bf16[1,1,512,4,128]{4,3,2,1,0:T(4,128)(2,1)} %get-tuple-element.24) | data formatting | bytes 1048576
  92.4 2.1 %copy.188 = bf16[1,1,512,4,128]{2,4,3,1,0:T(8,128)(2,1)} copy(bf16[1,1,512,4,128]{4,3,2,1,0:T(4,128)(2,1)} %get-tuple-element.32) | data formatting | bytes 1048576
  94.5 2.1 %copy.189 = bf16[1,1,512,4,128]{2,4,3,1,0:T(8,128)(2,1)} copy(bf16[1,1,512,4,128]{4,3,2,1,0:T(4,128)(2,1)} %get-tuple-element.23) | data formatting | bytes 1048576
  96.6 2.1 %copy.190 = bf16[1,1,512,4,128]{2,4,3,1,0:T(8,128)(2,1)} copy(bf16[1,1,512,4,128]{4,3,2,1,0:T(4,128)(2,1)} %get-tuple-element.31) | data formatting | bytes 1048576
  98.8 1.3 copy.145
  100.1 2.9 %divide_subtract_fusion.1 = (f32[1,512,4,128]{1,3,2,0:T(8,128)S(1)}, f32[1,512,4,128]{1,3,2,0:T(8,128)}) fusion(f32[1,512,4,128]{1,3,2,0:T(8,128)S(1)} %copy.179, f32[1,512,4,128]{1,3,2,0:T(8,128)} %bitcast.148, f32[512]{0:T(512)S(1)} %get-tuple-element.100, f32[512]{0:T(512)S(1)} %get-tuple-element.101, f32[512]{0:T(512)S(1)} %get-tuple-element.102, ...), kind=kLoop, calls=%fused_computation.95 | loop fusion | flops 3407872 | bytes 5257216 | tf_op jit(solution)/shard_map/sub | solution.py:81
  103.0 1.4 copy.146
  104.4 2.6 %copy.148 = f32[1,512,4,128]{3,2,1,0:T(4,128)} copy(f32[1,512,4,128]{1,3,2,0:T(8,128)} %get-tuple-element.48) | data formatting | bytes 2097152 | tf_op jit(solution)/shard_map/sub | solution.py:81
  107.1 2.8 %pad_maximum_fusion.5 = f32[2,512,4,128]{1,3,2,0:T(8,128)} fusion(f32[1,512,4,128]{1,3,2,0:T(8,128)} %get-tuple-element.48, f32[1,512,4,128]{1,3,2,0:T(8,128)S(1)} %get-tuple-element.47), kind=kLoop, calls=%fused_computation.39 | loop fusion | flops 524288 | bytes 4194304 | tf_op jit(solution)/shard_map/stack | solution.py:81
  109.8 2.9 %copy.149 = f32[2,512,4,128]{3,2,1,0:T(4,128)} copy(f32[2,512,4,128]{1,3,2,0:T(8,128)} %pad_maximum_fusion.5) | data formatting | bytes 4194304 | tf_op jit(solution)/shard_map/stack | solution.py:81
  112.8 5.3 %multiply_reduce_fusion = f32[4,2]{1,0:T(4,128)S(1)} fusion(bf16[4,2,512,4,128]{4,3,2,1,0:T(4,128)(2,1)} %param.13, f32[2,512,4,128]{3,2,1,0:T(4,128)} %copy.149), kind=kLoop, calls=%fused_computation | loop fusion | flops 6291448 | bytes 6291488 | tf_op jit(solution)/shard_map/reduce_sum | solution.py:83
  118.1 2.3 %fusion.15 = f32[2]{0:T(128)S(1)} fusion(f32[1,262144]{1,0:T(1,128)S(1)} %bitcast.146, f32[1,262144]{1,0:T(1,128)S(1)} %bitcast.145), kind=kLoop, calls=%fused_computation.38 | loop fusion | flops 1572862 | bytes 2097160 | tf_op jit(solution)/shard_map/reduce_sum | solution.py:84
  120.4 40.7 %all-reduce.1 = (f32[2,4,4]{2,1,0:T(4,128)S(1)}, f32[2,4]{0,1:T(4,128)S(1)}, f32[2]{0:T(128)S(1)}) all-reduce(f32[2,4,4]{2,1,0:T(4,128)S(1)} %fusion, f32[2,4]{0,1:T(4,128)S(1)} %bitcast.156, f32[2]{0:T(128)S(1)} %fusion.15), channel_id=1, replica_groups=mesh['egrp'=2,'space'=16] {'egrp','space'}, use_global_device_ids=true, to_apply=%region_4.5 | all-reduce | flops 42 | bytes 336 | tf_op jit(solution)/shard_map/psum | solution.py:88
  173.4 6.4 %bitcast_add_fusion = f32[1,512,4,128]{1,3,2,0:T(8,128)S(1)} fusion(bf16[1,1,512,4,128]{2,4,3,1,0:T(8,128)(2,1)} %copy.198, bf16[1,1,512,4,128]{2,4,3,1,0:T(8,128)(2,1)} %copy.197, bf16[1,1,512,4,128]{2,4,3,1,0:T(8,128)(2,1)} %copy.196, bf16[1,1,512,4,128]{2,4,3,1,0:T(8,128)(2,1)} %copy.195, bf16[1,1,512,4,128]{2,4,3,1,0:T(8,128)(2,1)} %copy.194, ...), kind=kLoop, calls=%fused_computation.87 | loop fusion | flops 9175040 | bytes 6303764 | tf_op jit(solution)/shard_map/add | solution.py:101
  179.9 4.2 %bitcast_add_fusion.4 = f32[1,512,4,128]{1,3,2,0:T(8,128)S(1)} fusion(bf16[1,1,512,4,128]{2,4,3,1,0:T(8,128)(2,1)S(1)} %copy-done.9, bf16[1,1,512,4,128]{2,4,3,1,0:T(8,128)(2,1)S(1)} %copy-done.8, bf16[1,1,512,4,128]{2,4,3,1,0:T(8,128)(2,1)S(1)} %copy-done.7, bf16[1,1,512,4,128]{2,4,3,1,0:T(8,128)(2,1)S(1)} %copy-done.6, ...), kind=kLoop, calls=%fused_computation.91 | loop fusion | flops 7077888 | bytes 7340052 | tf_op jit(solution)/shard_map/add | solution.py:101
  184.2 4.5 %collective-permute-start.1 = (f32[2,512,1,128]{1,3,2,0:T(8,128)S(1)}, f32[2,512,1,128]{1,3,2,0:T(8,128)S(1)}, u32[]{:S(2)}, u32[]{:S(2)}) collective-permute-start(f32[2,512,1,128]{1,3,2,0:T(8,128)S(1)} %get-tuple-element.41), channel_id=1, source_target_pairs={{0,1},{1,2},{2,3},{3,4},{4,5},{5,6},{6,7},{7,8},{8,9},{9,10},{10,1... | collective-permute-start | bytes 1572872 | tf_op jit(solution)/shard_map/ppermute | solution.py:18
  188.7 1.9 collective-permute-start.3
  191.4 9.0 %collective-permute-done.1 = f32[2,512,1,128]{1,3,2,0:T(8,128)S(1)} collective-permute-done((f32[2,512,1,128]{1,3,2,0:T(8,128)S(1)}, f32[2,512,1,128]{1,3,2,0:T(8,128)S(1)}, u32[]{:S(2)}, u32[]{:S(2)}) %collective-permute-start.1) | collective-permute-done | bytes 524320 | tf_op jit(solution)/shard_map/ppermute | solution.py:18
  200.4 1.6 collective-permute-done.3
  202.0 2.9 %fusion.11 = f32[2,512,4,128]{1,3,2,0:T(8,128)S(1)} fusion(f32[2,512,1,128]{1,3,2,0:T(8,128)S(1)} %collective-permute-done.3, f32[1,512,4,128]{1,3,2,0:T(8,128)S(1)} %bitcast_add_fusion, f32[1,512,4,128]{1,3,2,0:T(8,128)S(1)} %bitcast_add_fusion.4, f32[2,512,1,128]{1,3,2,0:T(8,128)S(1)} %collective-permute-done.1, ...), kind=kLoop, calls=%fused_computation.30 | loop fusion | flops 15204352 | bytes 11545096 | tf_op jit(solution)/shard_map/add | solution.py:27
  205.6 1.8 copy.178
  (94 shorter events, 16.4 us)
Async XLA Ops:
  3.5 4.9 %copy-start.10 = (f32[4,128]{1,0:T(4,128)S(1)}, f32[4,128]{1,0:T(4,128)}, u32[]{:S(2)}) copy-start(f32[4,128]{1,0:T(4,128)} %param.14) | copy-start | bytes 6148
  3.5 10.8 %copy-start.11 = (s32[4]{0:T(128)S(1)}, s32[4]{0:T(128)}, u32[]{:S(2)}) copy-start(s32[4]{0:T(128)} %param.16) | copy-start | bytes 52
  4.6 68.0 %all-to-all-start = ((f32[2,512,256]{2,1,0:T(8,128)}), f32[2,512,256]{2,1,0:T(8,128)S(1)}, u32[]{:S(2)}, u32[]{:S(2)}) async-start(f32[2,512,256]{2,1,0:T(8,128)} %pad_maximum_fusion.7), calls=%async_computation | async-start | bytes 2097152 | tf_op jit(solution)/shard_map/all_to_all | solution.py:53
  8.4 90.3 %collective-permute-start = (f32[1,1,1,128]{3,2,1,0:T(1,128)S(1)}, f32[1,1,1,128]{3,2,1,0:T(1,128)S(1)}, u32[]{:S(2)}, u32[]{:S(2)}) collective-permute-start(f32[1,1,1,128]{3,2,1,0:T(1,128)S(1)} %get-tuple-element.55), channel_id=1, source_target_pairs={{0,1},{1,2},{2,3},{3,4},{4,5},{5,6},{6,7},{7,8},{8,9},{9,10},{10,1... | collective-permute-start | bytes 1544 | tf_op jit(solution)/shard_map/ppermute | solution.py:18
  12.4 86.4 %collective-permute-start.2 = (f32[1,1,1,128]{3,2,1,0:T(1,128)S(1)}, f32[1,1,1,128]{3,2,1,0:T(1,128)S(1)}, u32[]{:S(2)}, u32[]{:S(2)}) collective-permute-start(f32[1,1,1,128]{3,2,1,0:T(1,128)S(1)} %get-tuple-element.56), channel_id=1, source_target_pairs={{1,0},{2,1},{3,2},{4,3},{5,4},{6,5},{7,6},{8,7},{9,8},{10,9},{11,1... | collective-permute-start | bytes 1544 | tf_op jit(solution)/shard_map/ppermute | solution.py:21
  30.6 4.4 %copy-start.12 = (f32[4]{0:T(128)S(1)}, f32[4]{0:T(128)}, u32[]{:S(2)}) copy-start(f32[4]{0:T(128)} %param.17) | copy-start | bytes 52
  30.6 10.2 %copy-start.13 = (s32[4,128]{1,0:T(4,128)S(1)}, s32[4,128]{1,0:T(4,128)}, u32[]{:S(2)}) copy-start(s32[4,128]{1,0:T(4,128)} %param.15) | copy-start | bytes 6148
  34.8 10.1 %copy-start.14 = (s32[2,4]{1,0:T(2,128)S(1)}, s32[2,4]{1,0:T(2,128)}, u32[]{:S(2)}) copy-start(s32[2,4]{1,0:T(2,128)} %param.18) | copy-start | bytes 100
  74.8 23.9 %all-to-all-start.1 = ((f32[2,512,256]{2,1,0:T(8,128)}), f32[2,512,256]{2,1,0:T(8,128)S(1)}, u32[]{:S(2)}, u32[]{:S(2)}) async-start(f32[2,512,256]{2,1,0:T(8,128)} %bitcast.144), calls=%async_computation.1 | async-start | bytes 2097152 | tf_op jit(solution)/shard_map/all_to_all | solution.py:75
  112.8 5.3 %copy-start = (f32[1,512,4,128]{3,2,1,0:T(4,128)S(1)}, f32[1,512,4,128]{3,2,1,0:T(4,128)}, u32[]{:S(2)}) copy-start(f32[1,512,4,128]{3,2,1,0:T(4,128)} %copy.146) | copy-start | bytes 3145732
  112.8 5.3 %copy-start.1 = (f32[1,512,4,128]{3,2,1,0:T(4,128)S(1)}, f32[1,512,4,128]{3,2,1,0:T(4,128)}, u32[]{:S(2)}) copy-start(f32[1,512,4,128]{3,2,1,0:T(4,128)} %copy.148) | copy-start | bytes 3145732
  173.4 6.5 %copy-start.2 = (bf16[1,1,512,4,128]{2,4,3,1,0:T(8,128)(2,1)S(1)}, bf16[1,1,512,4,128]{2,4,3,1,0:T(8,128)(2,1)}, u32[]{:S(2)}) copy-start(bf16[1,1,512,4,128]{2,4,3,1,0:T(8,128)(2,1)} %copy.183) | copy-start | bytes 1572868
  173.4 6.5 %copy-start.3 = (bf16[1,1,512,4,128]{2,4,3,1,0:T(8,128)(2,1)S(1)}, bf16[1,1,512,4,128]{2,4,3,1,0:T(8,128)(2,1)}, u32[]{:S(2)}) copy-start(bf16[1,1,512,4,128]{2,4,3,1,0:T(8,128)(2,1)} %copy.184) | copy-start | bytes 1572868
  173.4 6.5 %copy-start.4 = (bf16[1,1,512,4,128]{2,4,3,1,0:T(8,128)(2,1)S(1)}, bf16[1,1,512,4,128]{2,4,3,1,0:T(8,128)(2,1)}, u32[]{:S(2)}) copy-start(bf16[1,1,512,4,128]{2,4,3,1,0:T(8,128)(2,1)} %copy.185) | copy-start | bytes 1572868
  173.4 6.5 %copy-start.5 = (bf16[1,1,512,4,128]{2,4,3,1,0:T(8,128)(2,1)S(1)}, bf16[1,1,512,4,128]{2,4,3,1,0:T(8,128)(2,1)}, u32[]{:S(2)}) copy-start(bf16[1,1,512,4,128]{2,4,3,1,0:T(8,128)(2,1)} %copy.186) | copy-start | bytes 1572868
  173.4 6.5 %copy-start.6 = (bf16[1,1,512,4,128]{2,4,3,1,0:T(8,128)(2,1)S(1)}, bf16[1,1,512,4,128]{2,4,3,1,0:T(8,128)(2,1)}, u32[]{:S(2)}) copy-start(bf16[1,1,512,4,128]{2,4,3,1,0:T(8,128)(2,1)} %copy.187) | copy-start | bytes 1572868
  173.4 6.5 %copy-start.7 = (bf16[1,1,512,4,128]{2,4,3,1,0:T(8,128)(2,1)S(1)}, bf16[1,1,512,4,128]{2,4,3,1,0:T(8,128)(2,1)}, u32[]{:S(2)}) copy-start(bf16[1,1,512,4,128]{2,4,3,1,0:T(8,128)(2,1)} %copy.188) | copy-start | bytes 1572868
  173.4 6.5 %copy-start.8 = (bf16[1,1,512,4,128]{2,4,3,1,0:T(8,128)(2,1)S(1)}, bf16[1,1,512,4,128]{2,4,3,1,0:T(8,128)(2,1)}, u32[]{:S(2)}) copy-start(bf16[1,1,512,4,128]{2,4,3,1,0:T(8,128)(2,1)} %copy.189) | copy-start | bytes 1572868
  173.4 6.5 %copy-start.9 = (bf16[1,1,512,4,128]{2,4,3,1,0:T(8,128)(2,1)S(1)}, bf16[1,1,512,4,128]{2,4,3,1,0:T(8,128)(2,1)}, u32[]{:S(2)}) copy-start(bf16[1,1,512,4,128]{2,4,3,1,0:T(8,128)(2,1)} %copy.190) | copy-start | bytes 1572868
  184.2 16.2 %collective-permute-start.1 = (f32[2,512,1,128]{1,3,2,0:T(8,128)S(1)}, f32[2,512,1,128]{1,3,2,0:T(8,128)S(1)}, u32[]{:S(2)}, u32[]{:S(2)}) collective-permute-start(f32[2,512,1,128]{1,3,2,0:T(8,128)S(1)} %get-tuple-element.41), channel_id=1, source_target_pairs={{0,1},{1,2},{2,3},{3,4},{4,5},{5,6},{6,7},{7,8},{8,9},{9,10},{10,1... | collective-permute-start | bytes 1572872 | tf_op jit(solution)/shard_map/ppermute | solution.py:18
  188.7 13.3 %collective-permute-start.3 = (f32[2,512,1,128]{1,3,2,0:T(8,128)S(1)}, f32[2,512,1,128]{1,3,2,0:T(8,128)S(1)}, u32[]{:S(2)}, u32[]{:S(2)}) collective-permute-start(f32[2,512,1,128]{1,3,2,0:T(8,128)S(1)} %get-tuple-element.42), channel_id=1, source_target_pairs={{1,0},{2,1},{3,2},{4,3},{5,4},{6,5},{7,6},{8,7},{9,8},{10,9},{11,1... | collective-permute-start | bytes 1572872 | tf_op jit(solution)/shard_map/ppermute | solution.py:21
